TPU v7x, 32 devices: a whole 2x2x4 slice. The times are simulated.
32 devices in a mesh: ent: 8 (over z, y), rep: 4 (over x, core).
Axes of the slice: x: 2, y: 2, z: 4, core: 2. Of those that a mesh axis runs over, the one named last changes fastest.
Arguments:
- facts: bfloat16 [65536, 512], P(('ent', 'rep')), may hold values from -6 to 6
- fact_owner: int32 [65536, 1], P(('ent', 'rep')), may hold values from 0 to 7; in each aligned block of 2048 rows (0 to 2047, 2048 to 4095, ...) at most 512 rows name the same one
- fact_slot: int32 [65536], P(('ent', 'rep')), may hold values from 0 to 127
- entity_feats: bfloat16 [1024, 512], P('ent'), may hold values from -6 to 6
- out_cotangent: bfloat16 [1024, 512], P('ent'), may hold values from -6 to 6
- w_msg: bfloat16 [512, 512], replicated, may hold values from -0.25 to 0.25
- w_upd: bfloat16 [512, 512], replicated, may hold values from -0.25 to 0.25
Outputs:
- ent_out: bfloat16 [1024, 512], P('ent')
- fact_grad: bfloat16 [65536, 512], P(('ent', 'rep'))
- msg_weight_grad: float32 [512, 512], P(('ent', 'rep'))
- upd_weight_grad_t: float32 [512, 512], P(('ent', 'rep'))
Inputs may be any that keep to these rules, and one draw needn't show every extreme that they name: `fact_owner`: among the rows of one device, at most 512 name the same owner.
All inputs are finite; a program needn't handle non-finite values.
Results may differ from a plain program's by a relative error of at most 0.0065.
Values may be sent and summed in bfloat16 or wider, within the bound.
A program may use at most 64 MiB of HBM per device.

v0:
```python
import jax
import jax.numpy as jnp
from jax import lax
from jax.sharding import PartitionSpec as P


def silu_grad(value):
    sig = jax.nn.sigmoid(value)
    return sig * (1.0 + value * (1.0 - sig))


def per_device(facts, fact_owner, fact_slot, entity_feats, out_cotangent, w_msg, w_upd):
    n_owners = lax.axis_size("ent")
    n_copies = lax.axis_size("rep")
    width = facts.shape[1]
    ent_rows = entity_feats.shape[0]
    ents = ent_rows * n_owners
    share = ent_rows // n_copies
    key = fact_owner[:, 0] * ent_rows + fact_slot
    onehot = (jnp.arange(ents, dtype=jnp.int32)[:, None] == key[None, :]).astype(jnp.bfloat16)
    pre = jnp.dot(facts, w_msg, preferred_element_type=jnp.float32)
    message = jax.nn.silu(pre).astype(jnp.bfloat16)
    part_agg = jnp.dot(onehot, message, preferred_element_type=jnp.float32)
    part_count = jnp.sum(onehot, axis=1, dtype=jnp.float32)
    part = jnp.concatenate([part_agg, jnp.broadcast_to(part_count[:, None], (ents, 128))], axis=1)
    both = lax.psum_scatter(part, ("ent", "rep"), scatter_dimension=0, tiled=True)
    agg = both[:, :width]
    denom = jnp.maximum(both[:, width : width + 1], 1.0)
    begin = lax.axis_index("rep") * share
    feats = lax.dynamic_slice_in_dim(entity_feats, begin, share, 0)
    cot = lax.dynamic_slice_in_dim(out_cotangent, begin, share, 0)
    mean = (agg / denom).astype(jnp.bfloat16)
    zval = jnp.dot(mean, w_upd, preferred_element_type=jnp.float32)
    ent_part = (feats.astype(jnp.float32) + jax.nn.silu(zval)).astype(jnp.bfloat16)
    grad_z = (cot.astype(jnp.float32) * silu_grad(zval)).astype(jnp.bfloat16)
    d_mean = lax.dot_general(
        grad_z, w_upd, (((1,), (1,)), ((), ())), preferred_element_type=jnp.float32
    )
    d_agg = (d_mean / denom).astype(jnp.bfloat16)
    d_all = lax.all_gather(d_agg, ("ent", "rep"), axis=0, tiled=True)
    ent_out = lax.all_gather(ent_part, "rep", axis=0, tiled=True)
    d_msg = lax.dot_general(
        onehot, d_all, (((0,), (0,)), ((), ())), preferred_element_type=jnp.float32
    )
    d_pre = (d_msg * silu_grad(pre)).astype(jnp.bfloat16)
    fact_grad = lax.dot_general(
        d_pre, w_msg, (((1,), (1,)), ((), ())), preferred_element_type=jnp.float32
    ).astype(jnp.bfloat16)
    left = lax.dot_general(
        facts, d_pre, (((0,), (0,)), ((), ())), preferred_element_type=jnp.float32
    )
    right = lax.dot_general(
        grad_z, mean, (((0,), (0,)), ((), ())), preferred_element_type=jnp.float32
    )
    grads = lax.psum_scatter(
        jnp.concatenate([left, right], axis=1), ("ent", "rep"), scatter_dimension=0, tiled=True
    )
    return (ent_out, fact_grad, grads[:, :width], grads[:, width:])


def solution(mesh):
    placed = (
        P(("ent", "rep"), None),
        P(("ent", "rep"), None),
        P(("ent", "rep")),
        P("ent", None),
        P("ent", None),
        P(),
        P(),
    )
    return jax.shard_map(
        per_device,
        mesh=mesh,
        in_specs=placed,
        out_specs=(
            P("ent", None),
            P(("ent", "rep"), None),
            P(("ent", "rep"), None),
            P(("ent", "rep"), None),
        ),
        check_vma=False,
    )
```

profile of v0, /device:TPU:0, one launch (start us, length us, event | category | flops | bytes accessed | tf_op | source)
XLA Modules:
  0.0 369.4 jit_solution(3396001357918936834)
XLA Ops:
  7.2 0.0 copy-start
  7.2 0.0 reduce-scatter.7.cloned.1.call-start
  7.2 0.8 broadcast_multiply_fusion
  8.1 0.7 add.31
  8.8 0.9 convert_reduce_fusion
  9.7 0.0 copy-done
  9.7 2.3 fusion.13
  12.0 0.0 copy-start.1
  12.0 2.8 fusion.2
  14.8 0.0 copy-done.1
  14.9 1.9 pad_maximum_fusion
  16.8 3.3 copy.19
  20.1 0.0 copy-start.4
  20.1 0.0 copy-start.3
  20.1 0.0 reduce-scatter.7.cloned.1.call-update
  20.1 0.0 all-gather.2.cloned.1.call-start
  20.2 140.3 %reduce-scatter.7.cloned.1.call-done = f32[32,640]{1,0:T(8,128)} async-done(((f32[1024,640]{1,0:T(8,128)}), f32[32,640]{1,0:T(8,128)}) %reduce-scatter.7.cloned.1.call-update) | async-done | bytes 81936 | tf_op jit(solution)/shard_map/reduce_scatter | solution.py:26
  160.5 0.7 slice_maximum_fusion
  161.2 0.1 copy.26
  161.3 0.0 copy-done.4
  161.3 1.1 add_convert_fusion
  162.4 0.0 copy-done.3
  162.4 0.9 fusion.5
  163.3 0.0 all-gather.2.cloned.1.call-update
  163.3 0.0 reduce-scatter.9.cloned.1.call-start
  163.4 1.3 fusion.8
  164.6 48.9 %all-gather.2.cloned.1.call-done = bf16[1024,512]{1,0:T(8,128)(2,1)} async-done(((bf16[32,512]{1,0:T(8,128)(2,1)}), bf16[1024,512]{1,0:T(8,128)(2,1)}) %all-gather.2.cloned.1.call-update) | async-done | bytes 1048592 | tf_op jit(solution)/shard_map/all_gather | solution.py:40
  213.5 6.1 %multiply_convert_fusion = bf16[2048,512]{1,0:T(8,128)(2,1)S(1)} fusion(f32[2048,512]{1,0:T(8,128)} %copy-done.1, bf16[1024,512]{1,0:T(8,128)(2,1)} %all-gather.2.cloned.1.call-done, s32[2048]{0:T(1024)S(1)} %add.31), kind=kOutput, calls=%fused_computation.5 | convolution fusion | flops 2159017984 | bytes 7348224 | tf_op jit(solution)/shard_map/dot_general | solution.py:42
  219.6 0.0 copy-start.5
  219.6 1.3 convolution_bitcast_fusion
  220.9 0.0 copy-done.5
  221.0 1.5 pad_maximum_fusion.1
  222.4 0.0 copy-start.2
  222.4 2.9 copy.21
  225.4 0.0 reduce-scatter.9.cloned.1.call-update
  225.4 5.4 %all_gather.6 = bf16[128,512]{1,0:T(8,128)(2,1)S(1)} all-gather(bf16[32,512]{1,0:T(8,128)(2,1)S(1)} %get-tuple-element.18), channel_id=1, replica_groups=mesh['ent'=8,'rep'=4] {'rep'}, dimensions={0}, use_global_device_ids=true | all-gather | bytes 163840 | tf_op jit(solution)/shard_map/all_gather | solution.py:41
  230.8 0.0 copy-done.2
  230.8 4.2 %convolution_convert_fusion = bf16[2048,512]{1,0:T(8,128)(2,1)} fusion(bf16[2048,512]{1,0:T(8,128)(2,1)} %copy-done.5, bf16[512,512]{1,0:T(8,128)(2,1)S(1)} %copy-done.2), kind=kOutput, calls=%fused_computation.10 | convolution fusion | flops 1074790400 | bytes 4718592 | tf_op jit(solution)/shard_map/dot_general | solution.py:46
  235.0 125.8 %reduce-scatter.9.cloned.1.call-done = f32[16,1024]{1,0:T(8,128)} async-done(((f32[512,1024]{1,0:T(8,128)}), f32[16,1024]{1,0:T(8,128)}) %reduce-scatter.9.cloned.1.call-update) | async-done | bytes 65552
  360.8 1.4 fusion.12
  362.2 0.7 copy.28
  (1 shorter events, 0.0 us)
Async XLA Ops:
  7.2 2.5 copy-start
  7.2 153.3 %reduce-scatter.7.cloned.1.call-start = ((), (), s32[]{:S(2)}) async-start(), calls=%async_computation.3 | async-start | bytes 2703360 | tf_op jit(solution)/shard_map/reduce_scatter | solution.py:26
  12.0 2.8 copy-start.1
  20.1 141.2 %copy-start.4 = (bf16[512,512]{1,0:T(8,128)(2,1)S(1)}, bf16[512,512]{1,0:T(8,128)(2,1)}, u32[]{:S(2)}) copy-start(bf16[512,512]{1,0:T(8,128)(2,1)} %param.13) | copy-start | bytes 1572868
  20.1 142.3 %copy-start.3 = (bf16[128,512]{1,0:T(8,128)(2,1)S(1)}, bf16[128,512]{1,0:T(8,128)(2,1)}, u32[]{:S(2)}) copy-start(bf16[128,512]{1,0:T(8,128)(2,1)} %param.11) | copy-start | bytes 393220
  20.1 193.4 %all-gather.2.cloned.1.call-start = ((), (), s32[]{:S(2)}) async-start(), calls=%async_computation.2 | async-start | bytes 1081344 | tf_op jit(solution)/shard_map/all_gather | solution.py:40
  163.3 197.5 %reduce-scatter.9.cloned.1.call-start = ((), (), s32[]{:S(2)}) async-start(), calls=%async_computation.4 | async-start | bytes 2162688
  219.6 1.3 copy-start.5
  222.4 8.4 %copy-start.2 = (bf16[512,512]{1,0:T(8,128)(2,1)S(1)}, bf16[512,512]{1,0:T(8,128)(2,1)}, u32[]{:S(2)}) copy-start(bf16[512,512]{1,0:T(8,128)(2,1)} %param.12) | copy-start | bytes 1572868
Sparse Core Ops, SparseCore 0:
  20.2 140.2 reduce-scatter.6
  163.9 49.5 all-gather.1
  225.5 135.2 reduce-scatter.8
where the time goes:
time: 370 us; the launch traced here: 369 us
  waiting for transfers between devices  315 us (85%)
  matrix products  19.9 us (5%)
  between operations  13.8 us (4%)
  local copies, waits for them, and re-layouts  8.47 us (2%)
  other arithmetic  6.59 us (2%)
  blocking collectives  5.43 us (1%)
    reduce_scatter x1, waiting for transfers between devices, per_device(): lax.psum_scatter(part, ('ent', 'rep'), scatter_dimension=0, tiled=True)  140 us
    unnamed x4, waiting for transfers between devices  126 us
    all_gather x1, waiting for transfers between devices, per_device(): d_all = lax.all_gather(d_agg, ('ent', 'rep'), axis=0, tiled=True)  48.9 us
  transfers between devices with their start and end apart: 3, of which 3 were waited for; matrix products, arithmetic and copies ran while one was open for 1% of the time, Pallas kernels for 0%

commit v1 on v0

--- a/solution.py
+++ b/solution.py
@@ -37,7 +37,15 @@
         grad_z, w_upd, (((1,), (1,)), ((), ())), preferred_element_type=jnp.float32
     )
     d_agg = (d_mean / denom).astype(jnp.bfloat16)
-    d_all = lax.all_gather(d_agg, ("ent", "rep"), axis=0, tiled=True)
+    ways, here = (lax.axis_size(("ent", "rep")), lax.axis_index(("ent", "rep")))
+    grown, reach = (d_agg, 1)
+    while reach < ways:
+        theirs = lax.ppermute(grown, ("ent", "rep"), [(d, d ^ reach) for d in range(ways)])
+        mine_first = jnp.concatenate([grown, theirs], axis=0)
+        theirs_first = jnp.concatenate([theirs, grown], axis=0)
+        grown = jnp.where(here & reach == 0, mine_first, theirs_first)
+        reach = 2 * reach
+    d_all = grown
     ent_out = lax.all_gather(ent_part, "rep", axis=0, tiled=True)
     d_msg = lax.dot_general(
         onehot, d_all, (((0,), (0,)), ((), ())), preferred_element_type=jnp.float32

time: 370 us -> 360 us (0.973)
  waiting for transfers between devices: 315 us -> 304 us
    all_gather x1 -> x0, waiting for transfers between devices: 48.9 us -> none  [per_device(): d_all = lax.all_gather(d_agg, ('ent', 'rep'), axis=0, tiled=True)]
    ppermute x0 -> x5, waiting for transfers between devices: none -> 38.7 us  [per_device(): lax.ppermute(grown, ('ent', 'rep'), [(d, d ^ reach) for d in range(ways)])]
    unnamed x4 -> x3, waiting for transfers between devices: 126 us -> 125 us
  transfers between devices with their start and end apart: 3 -> 7, of which waited for: 3 -> 7; matrix products, arithmetic and copies ran while one was open for 1% -> 1% of each run, Pallas kernels for 0% -> 0%
where the time goes in v1:
time: 360 us
  waiting for transfers between devices  304 us (84%)
  matrix products  19.5 us (5%)
  between operations  14.2 us (4%)
  local copies, waits for them, and re-layouts  8.43 us (2%)
  other arithmetic  6.97 us (2%)
  blocking collectives  5.92 us (2%)
    reduce_scatter x1, waiting for transfers between devices, per_device(): lax.psum_scatter(part, ('ent', 'rep'), scatter_dimension=0, tiled=True)  140 us
    unnamed x3, waiting for transfers between devices  125 us
    ppermute x5, waiting for transfers between devices, per_device(): lax.ppermute(grown, ('ent', 'rep'), [(d, d ^ reach) for d in range(ways)])  38.7 us
  transfers between devices with their start and end apart: 7, of which 7 were waited for; matrix products, arithmetic and copies ran while one was open for 1% of the time, Pallas kernels for 0%

profile of v1, /device:TPU:0, one launch (start us, length us, event | category | flops | bytes accessed | tf_op | source)
XLA Modules:
  0.0 359.8 jit_solution(16743565029354760828)
XLA Ops:
  7.2 0.0 copy-start
  7.2 0.0 reduce-scatter.7.cloned.1.call-start
  7.2 0.8 broadcast_multiply_fusion
  8.1 0.7 add.34
  8.8 0.9 convert_reduce_fusion
  9.7 0.0 copy-done
  9.7 2.3 fusion.20
  12.0 0.0 copy-start.1
  12.0 2.8 fusion.2
  14.8 0.0 copy-done.1
  14.9 1.9 pad_maximum_fusion
  16.8 3.3 copy.20
  20.1 0.0 copy-start.5
  20.1 0.0 copy-start.4
  20.1 0.0 reduce-scatter.7.cloned.1.call-update
  20.1 0.0 reduce-scatter.9.cloned.1.call-start
  20.2 140.5 %reduce-scatter.7.cloned.1.call-done = f32[32,640]{1,0:T(8,128)} async-done(((f32[1024,640]{1,0:T(8,128)}), f32[32,640]{1,0:T(8,128)}) %reduce-scatter.7.cloned.1.call-update) | async-done | bytes 81936 | tf_op jit(solution)/shard_map/reduce_scatter | solution.py:26
  160.6 0.0 copy-start.3
  160.6 0.8 slice_maximum_fusion
  161.4 0.1 copy.27
  161.5 0.0 copy-done.5
  161.5 1.1 add_convert_fusion
  162.6 0.0 copy-done.4
  162.6 0.2 fusion.5
  162.9 0.1 collective-permute-start
  163.0 1.2 collective-permute-done
  164.2 0.1 collective-permute-start.1
  164.3 4.2 %collective-permute-done.1 = bf16[64,512]{1,0:T(8,128)(2,1)S(1)} collective-permute-done((bf16[64,512]{1,0:T(8,128)(2,1)S(1)}, bf16[64,512]{1,0:T(8,128)(2,1)S(1)}, u32[]{:S(2)}, u32[]{:S(2)}) %collective-permute-start.1) | collective-permute-done | bytes 65568 | tf_op jit(solution)/shard_map/ppermute | solution.py:43
  168.6 0.1 collective-permute-start.2
  168.6 4.9 %collective-permute-done.2 = bf16[128,512]{1,0:T(8,128)(2,1)S(1)} collective-permute-done((bf16[128,512]{1,0:T(8,128)(2,1)S(1)}, bf16[128,512]{1,0:T(8,128)(2,1)S(1)}, u32[]{:S(2)}, u32[]{:S(2)}) %collective-permute-start.2) | collective-permute-done | bytes 131104 | tf_op jit(solution)/shard_map/ppermute | solution.py:43
  173.6 0.1 maximum_select_fusion.3
  173.6 0.1 collective-permute-start.3
  173.7 6.4 %collective-permute-done.3 = bf16[256,512]{1,0:T(8,128)(2,1)S(1)} collective-permute-done((bf16[256,512]{1,0:T(8,128)(2,1)S(1)}, bf16[256,512]{1,0:T(8,128)(2,1)S(1)}, u32[]{:S(2)}, u32[]{:S(2)}) %collective-permute-start.3) | collective-permute-done | bytes 262176 | tf_op jit(solution)/shard_map/ppermute | solution.py:43
  180.1 0.2 maximum_select_fusion.2
  180.3 0.1 collective-permute-start.4
  180.4 0.0 copy-done.3
  180.4 0.4 fusion.15
  180.8 21.9 %collective-permute-done.4 = bf16[512,512]{1,0:T(8,128)(2,1)S(1)} collective-permute-done((bf16[512,512]{1,0:T(8,128)(2,1)S(1)}, bf16[512,512]{1,0:T(8,128)(2,1)S(1)}, u32[]{:S(2)}, u32[]{:S(2)}) %collective-permute-start.4) | collective-permute-done | bytes 524320 | tf_op jit(solution)/shard_map/ppermute | solution.py:43
  202.8 7.1 %multiply_convert_fusion = bf16[2048,512]{1,0:T(8,128)(2,1)S(1)} fusion(f32[2048,512]{1,0:T(8,128)} %copy-done.1, s32[2048]{0:T(1024)S(1)} %add.34, bf16[512,512]{1,0:T(8,128)(2,1)S(1)} %collective-permute-done.4, bf16[512,512]{1,0:T(8,128)(2,1)S(1)} %maximum_select_fusion.2, pred[]{:T(512)S(6)} %eq.31), kind=kOutput, calls=%fused_computation.5 | convolution fusion | flops 2163736576 | bytes 7348225 | tf_op jit(solution)/shard_map/dot_general | solution.py:50
  209.9 0.0 copy-start.6
  209.9 1.3 convolution_bitcast_fusion
  211.2 0.0 copy-done.6
  211.2 1.5 pad_maximum_fusion.1
  212.7 2.9 copy.22
  215.6 0.0 copy-start.2
  215.6 0.0 reduce-scatter.9.cloned.1.call-update
  215.7 5.9 %all_gather.3 = bf16[128,512]{1,0:T(8,128)(2,1)S(1)} all-gather(bf16[32,512]{1,0:T(8,128)(2,1)S(1)} %get-tuple-element.18), channel_id=1, replica_groups=mesh['ent'=8,'rep'=4] {'rep'}, dimensions={0}, use_global_device_ids=true | all-gather | bytes 163840 | tf_op jit(solution)/shard_map/all_gather | solution.py:49
  221.6 0.0 copy-done.2
  221.6 4.2 %convolution_convert_fusion = bf16[2048,512]{1,0:T(8,128)(2,1)} fusion(bf16[2048,512]{1,0:T(8,128)(2,1)} %copy-done.6, bf16[512,512]{1,0:T(8,128)(2,1)S(1)} %copy-done.2), kind=kOutput, calls=%fused_computation.10 | convolution fusion | flops 1074790400 | bytes 4718592 | tf_op jit(solution)/shard_map/dot_general | solution.py:54
  225.8 125.1 %reduce-scatter.9.cloned.1.call-done = f32[16,1024]{1,0:T(8,128)} async-done(((f32[512,1024]{1,0:T(8,128)}), f32[16,1024]{1,0:T(8,128)}) %reduce-scatter.9.cloned.1.call-update) | async-done | bytes 65552
  350.9 1.4 fusion.19
  352.3 0.7 copy.29
  (3 shorter events, 0.1 us)
Async XLA Ops:
  7.2 2.5 copy-start
  7.2 153.5 %reduce-scatter.7.cloned.1.call-start = ((), (), s32[]{:S(2)}) async-start(), calls=%async_computation.2 | async-start | bytes 2703360 | tf_op jit(solution)/shard_map/reduce_scatter | solution.py:26
  12.0 2.8 copy-start.1
  20.1 141.4 %copy-start.5 = (bf16[512,512]{1,0:T(8,128)(2,1)S(1)}, bf16[512,512]{1,0:T(8,128)(2,1)}, u32[]{:S(2)}) copy-start(bf16[512,512]{1,0:T(8,128)(2,1)} %param.13) | copy-start | bytes 1572868
  20.1 142.6 %copy-start.4 = (bf16[128,512]{1,0:T(8,128)(2,1)S(1)}, bf16[128,512]{1,0:T(8,128)(2,1)}, u32[]{:S(2)}) copy-start(bf16[128,512]{1,0:T(8,128)(2,1)} %param.11) | copy-start | bytes 393220
  20.1 330.8 %reduce-scatter.9.cloned.1.call-start = ((), (), s32[]{:S(2)}) async-start(), calls=%async_computation.3 | async-start | bytes 2162688
  160.6 19.7 %copy-start.3 = (f32[32,640]{1,0:T(8,128)S(1)}, f32[32,640]{1,0:T(8,128)}, u32[]{:S(2)}) copy-start(f32[32,640]{1,0:T(8,128)} %reduce-scatter.7.cloned.1.call-done) | copy-start | bytes 245764
  162.9 1.3 collective-permute-start
  164.2 4.3 %collective-permute-start.1 = (bf16[64,512]{1,0:T(8,128)(2,1)S(1)}, bf16[64,512]{1,0:T(8,128)(2,1)S(1)}, u32[]{:S(2)}, u32[]{:S(2)}) collective-permute-start(bf16[64,512]{1,0:T(8,128)(2,1)S(1)} %maximum_select_fusion.5), channel_id=1, source_target_pairs={{0,2},{1,3},{2,0},{3,1},{4,6},{5,7},{6,4},{7,5},{8,10},{9,11},{10,... | collective-permute-start | bytes 196616 | tf_op jit(solution)/shard_map/ppermute | solution.py:43
  168.6 5.0 %collective-permute-start.2 = (bf16[128,512]{1,0:T(8,128)(2,1)S(1)}, bf16[128,512]{1,0:T(8,128)(2,1)S(1)}, u32[]{:S(2)}, u32[]{:S(2)}) collective-permute-start(bf16[128,512]{1,0:T(8,128)(2,1)S(1)} %maximum_select_fusion.4), channel_id=1, source_target_pairs={{0,4},{1,5},{2,6},{3,7},{4,0},{5,1},{6,2},{7,3},{8,12},{9,13},{10,... | collective-permute-start | bytes 393224 | tf_op jit(solution)/shard_map/ppermute | solution.py:43
  173.6 6.4 %collective-permute-start.3 = (bf16[256,512]{1,0:T(8,128)(2,1)S(1)}, bf16[256,512]{1,0:T(8,128)(2,1)S(1)}, u32[]{:S(2)}, u32[]{:S(2)}) collective-permute-start(bf16[256,512]{1,0:T(8,128)(2,1)S(1)} %maximum_select_fusion.3), channel_id=1, source_target_pairs={{0,8},{1,9},{2,10},{3,11},{4,12},{5,13},{6,14},{7,15},{8,0},{9,1},... | collective-permute-start | bytes 786440 | tf_op jit(solution)/shard_map/ppermute | solution.py:43
  180.3 22.5 %collective-permute-start.4 = (bf16[512,512]{1,0:T(8,128)(2,1)S(1)}, bf16[512,512]{1,0:T(8,128)(2,1)S(1)}, u32[]{:S(2)}, u32[]{:S(2)}) collective-permute-start(bf16[512,512]{1,0:T(8,128)(2,1)S(1)} %maximum_select_fusion.2), channel_id=1, source_target_pairs={{0,16},{1,17},{2,18},{3,19},{4,20},{5,21},{6,22},{7,23},{8,24},{9,... | collective-permute-start | bytes 1572872 | tf_op jit(solution)/shard_map/ppermute | solution.py:43
  209.9 1.3 copy-start.6
  215.6 5.9 %copy-start.2 = (bf16[512,512]{1,0:T(8,128)(2,1)S(1)}, bf16[512,512]{1,0:T(8,128)(2,1)}, u32[]{:S(2)}) copy-start(bf16[512,512]{1,0:T(8,128)(2,1)} %param.12) | copy-start | bytes 1572868
Sparse Core Ops, SparseCore 0:
  20.2 140.3 reduce-scatter.6
  215.8 135.0 reduce-scatter.8
